TPU v7x, 32 devices: a whole 2x2x4 slice. The times are simulated.
32 devices in a mesh: rep: 2 (over x), shard: 16 (over z, y, core).
Axes of the slice: x: 2, y: 2, z: 4, core: 2. Of those that a mesh axis runs over, the one named last changes fastest.
Arguments:
- inputs: bfloat16 [32, 1024, 768], P(('rep', 'shard')), may hold values from -6 to 6
- doc_ids: int32 [32, 1024], P(('rep', 'shard')), may hold values from 0 to 3, never falling along the last dimension, each value on 1 to 512 neighbouring positions
- attn_gain: bfloat16 [768], P('shard'), may hold values from 0.25 to 1.75
- w_query: bfloat16 [768, 768], P('shard'), may hold values from -0.21875 to 0.21875
- w_key: bfloat16 [768, 768], P('shard'), may hold values from -0.21875 to 0.21875
- w_value: bfloat16 [768, 768], P('shard'), may hold values from -0.21875 to 0.21875
- w_out: bfloat16 [768, 768], P('shard'), may hold values from -1.75 to 1.75
- ffn_gain: bfloat16 [768], P('shard'), may hold values from 0.25 to 1.75
- w_gate: bfloat16 [768, 2048], P('shard'), may hold values from -0.21875 to 0.21875
- w_up: bfloat16 [768, 2048], P('shard'), may hold values from -0.21875 to 0.21875
- w_down: bfloat16 [2048, 768], P('shard'), may hold values from -0.125 to 0.125
- cotangent: bfloat16 [32, 1024, 768], P(('rep', 'shard')), may hold values from -6 to 6
Outputs:
- output: bfloat16 [32, 1024, 768], P(('rep', 'shard'))
- grad_input: float32 [32, 1024, 768], P(('rep', 'shard'))
- grad_attn_gain: float32 [768], P('shard')
- grad_w_query: float32 [768, 768], P('shard')
- grad_w_key: float32 [768, 768], P('shard')
- grad_w_value: float32 [768, 768], P('shard')
- grad_w_out: float32 [768, 768], P('shard')
- grad_ffn_gain: float32 [768], P('shard')
- grad_w_gate: float32 [768, 2048], P('shard')
- grad_w_up: float32 [768, 2048], P('shard')
- grad_w_down: float32 [2048, 768], P('shard')
Inputs may be any that keep to these rules, and one draw needn't show every extreme that they name: `doc_ids`: within a sequence document numbers never fall; every document has 1 to 512 tokens, and one has exactly 512.
All inputs are finite; a program needn't handle non-finite values.
Results may differ from a plain program's by a relative error of at most 0.017.
Values may be sent and summed in bfloat16 or wider, within the bound.
No kernel may reach another device: no remote copies, remote signals or barrier semaphores. Data moves between devices by JAX's collectives and lax.ppermute only.
A program may use at most 320 MiB of HBM per device.

v0:
```python
import jax
import jax.numpy as jnp
from jax import lax
from jax.sharding import PartitionSpec as P

H = 12
HD = 64
BLOCK = 256
epsilon = 1e-06
rope_base = 10000.0
masked_score = -1e30


def rope_tables(length, head_size):
    position = jnp.arange(length, dtype=jnp.float32)
    exponent = jnp.arange(head_size // 2, dtype=jnp.float32) * (2.0 / head_size)
    angles = position[:, None] * jnp.power(rope_base, -exponent)[None, :]
    return (jnp.cos(angles)[:, None, :], jnp.sin(angles)[:, None, :])


def rotate(tensor, cosine_table, sine_table):
    midway = tensor.shape[-1] // 2
    front_half = tensor[..., :midway]
    back_half = tensor[..., midway:]
    return jnp.concatenate(
        [
            front_half * cosine_table - back_half * sine_table,
            back_half * cosine_table + front_half * sine_table,
        ],
        axis=-1,
    )


def rotate_back(tensor, cosine_table, sine_table):
    midway = tensor.shape[-1] // 2
    front_half = tensor[..., :midway]
    back_half = tensor[..., midway:]
    return jnp.concatenate(
        [
            front_half * cosine_table + back_half * sine_table,
            back_half * cosine_table - front_half * sine_table,
        ],
        axis=-1,
    )


def allowed_pairs(doc_ids, offset, row_step, block_size):
    length = doc_ids.shape[1]
    row_docs = lax.dynamic_slice_in_dim(doc_ids, offset, row_step, 1)
    row_block = (offset + jnp.arange(row_step, dtype=jnp.int32)) // block_size
    col_block = jnp.arange(length, dtype=jnp.int32) // block_size
    same_doc = row_docs[:, :, None] == doc_ids[:, None, :]
    ordered = col_block[None, None, :] <= row_block[None, :, None]
    return (same_doc & ordered)[:, None, :, :]


def rows_product(left, right):
    return lax.dot_general(
        left, right, (((0,), (0,)), ((), ())), preferred_element_type=jnp.float32
    )


def right_transposed(left, right):
    return lax.dot_general(
        left, right, (((1,), (1,)), ((), ())), preferred_element_type=jnp.float32
    )


def norm_back(grad_normed, normed, inverse):
    return inverse * (grad_normed - normed * jnp.mean(grad_normed * normed, -1, keepdims=True))


def block_scores(query_block, keys_rot, doc_ids, offset, row_step, factor):
    allowed = allowed_pairs(doc_ids, offset, row_step, BLOCK)
    scores = (
        jnp.einsum("bqhd,bkhd->bhqk", query_block, keys_rot, preferred_element_type=jnp.float32)
        * factor
    )
    return jnp.where(allowed, scores, masked_score)


def per_device(
    inputs,
    doc_ids,
    attn_gain,
    w_query,
    w_key,
    w_value,
    w_out,
    ffn_gain,
    w_gate,
    w_up,
    w_down,
    cotangent,
):
    batch_size, length, model_width = inputs.shape
    rows_total = batch_size * length
    head_count = H
    head_size = HD
    row_step = min(512, length)
    factor = head_size ** (-0.5)
    gain_one, query_mat, key_mat, value_mat, out_mat, gain_two, gate_mat, up_mat, down_mat = (
        lax.all_gather(attn_gain, "shard", axis=0, tiled=True),
        lax.all_gather(w_query, "shard", axis=0, tiled=True),
        lax.all_gather(w_key, "shard", axis=0, tiled=True),
        lax.all_gather(w_value, "shard", axis=0, tiled=True),
        lax.all_gather(w_out, "shard", axis=0, tiled=True),
        lax.all_gather(ffn_gain, "shard", axis=0, tiled=True),
        lax.all_gather(w_gate, "shard", axis=0, tiled=True),
        lax.all_gather(w_up, "shard", axis=0, tiled=True),
        lax.all_gather(w_down, "shard", axis=0, tiled=True),
    )
    resid = inputs.astype(jnp.float32).reshape(rows_total, model_width)
    inv_one = lax.rsqrt(jnp.mean(resid * resid, -1, keepdims=True) + epsilon)
    normed_one = resid * inv_one
    gain_first = gain_one.astype(jnp.float32)
    attn_in = (normed_one * gain_first).astype(jnp.bfloat16)
    cosine_table, sine_table = rope_tables(length, head_size)

    def project(matrix):
        return jnp.dot(attn_in, matrix, preferred_element_type=jnp.float32).reshape(
            batch_size, length, head_count, head_size
        )

    queries = rotate(project(query_mat), cosine_table, sine_table).astype(jnp.bfloat16)
    keys_rot = rotate(project(key_mat), cosine_table, sine_table).astype(jnp.bfloat16)
    value_vec = project(value_mat).astype(jnp.bfloat16)
    mixed_blocks = []
    log_sums = []
    for offset in range(0, length, row_step):
        query_block = queries[:, offset : offset + row_step]
        scores = block_scores(query_block, keys_rot, doc_ids, offset, row_step, factor)
        row_peak = jnp.max(scores, -1, keepdims=True)
        exp_scores = jnp.exp(scores - row_peak)
        row_total = jnp.sum(exp_scores, -1, keepdims=True)
        attn_probs = (exp_scores / row_total).astype(jnp.bfloat16)
        log_sums.append(row_peak + jnp.log(row_total))
        mixed_blocks.append(
            jnp.einsum("bhqk,bkhd->bqhd", attn_probs, value_vec, preferred_element_type=jnp.float32)
        )
    mixed_heads = (
        jnp.concatenate(mixed_blocks, 1).reshape(rows_total, model_width).astype(jnp.bfloat16)
    )
    middle = resid + jnp.dot(mixed_heads, out_mat, preferred_element_type=jnp.float32)
    inv_two = lax.rsqrt(jnp.mean(middle * middle, -1, keepdims=True) + epsilon)
    normed_two = middle * inv_two
    gain_second = gain_two.astype(jnp.float32)
    ffn_in = (normed_two * gain_second).astype(jnp.bfloat16)
    gate_pre = jnp.dot(ffn_in, gate_mat, preferred_element_type=jnp.float32)
    up_pre = jnp.dot(ffn_in, up_mat, preferred_element_type=jnp.float32)
    gate_sigmoid = jax.nn.sigmoid(gate_pre)
    hidden = (gate_pre * gate_sigmoid * up_pre).astype(jnp.bfloat16)
    result = middle + jnp.dot(hidden, down_mat, preferred_element_type=jnp.float32)
    output = result.astype(jnp.bfloat16).reshape(batch_size, length, model_width)
    gain_one, query_mat, key_mat, value_mat, out_mat, gain_two, gate_mat, up_mat, down_mat = (
        lax.all_gather(attn_gain, "shard", axis=0, tiled=True),
        lax.all_gather(w_query, "shard", axis=0, tiled=True),
        lax.all_gather(w_key, "shard", axis=0, tiled=True),
        lax.all_gather(w_value, "shard", axis=0, tiled=True),
        lax.all_gather(w_out, "shard", axis=0, tiled=True),
        lax.all_gather(ffn_gain, "shard", axis=0, tiled=True),
        lax.all_gather(w_gate, "shard", axis=0, tiled=True),
        lax.all_gather(w_up, "shard", axis=0, tiled=True),
        lax.all_gather(w_down, "shard", axis=0, tiled=True),
    )
    branch_grad = cotangent.reshape(rows_total, model_width)
    grad_out = branch_grad.astype(jnp.float32)
    grad_w_down = rows_product(hidden, branch_grad)
    grad_hidden = right_transposed(branch_grad, down_mat)
    grad_gate = (
        grad_hidden * up_pre * gate_sigmoid * (1.0 + gate_pre * (1.0 - gate_sigmoid))
    ).astype(jnp.bfloat16)
    grad_up = (grad_hidden * gate_pre * gate_sigmoid).astype(jnp.bfloat16)
    grad_w_gate = rows_product(ffn_in, grad_gate)
    grad_w_up = rows_product(ffn_in, grad_up)
    grad_ffn_in = right_transposed(grad_gate, gate_mat) + right_transposed(grad_up, up_mat)
    grad_gain_two = jnp.sum(grad_ffn_in * normed_two, 0)
    grad_middle = grad_out + norm_back(grad_ffn_in * gain_second, normed_two, inv_two)
    attn_grad = grad_middle.astype(jnp.bfloat16)
    grad_w_out = rows_product(mixed_heads, attn_grad)
    grad_mixed = (
        right_transposed(attn_grad, out_mat)
        .astype(jnp.bfloat16)
        .reshape(batch_size, length, head_count, head_size)
    )
    grad_key = jnp.zeros((batch_size, length, head_count, head_size), jnp.float32)
    grad_value = jnp.zeros((batch_size, length, head_count, head_size), jnp.float32)
    grad_query_blocks = []
    for block_index, offset in enumerate(range(0, length, row_step)):
        query_block = queries[:, offset : offset + row_step]
        scores = block_scores(query_block, keys_rot, doc_ids, offset, row_step, factor)
        probs_full = jnp.exp(scores - log_sums[block_index])
        attn_probs = probs_full.astype(jnp.bfloat16)
        grad_block = grad_mixed[:, offset : offset + row_step]
        grad_value = grad_value + jnp.einsum(
            "bhqk,bqhd->bkhd", attn_probs, grad_block, preferred_element_type=jnp.float32
        )
        grad_probs = jnp.einsum(
            "bqhd,bkhd->bhqk", grad_block, value_vec, preferred_element_type=jnp.float32
        )
        grad_scores = (
            probs_full * (grad_probs - jnp.sum(probs_full * grad_probs, -1, keepdims=True))
        ).astype(jnp.bfloat16)
        grad_query_blocks.append(
            jnp.einsum("bhqk,bkhd->bqhd", grad_scores, keys_rot, preferred_element_type=jnp.float32)
            * factor
        )
        grad_key = (
            grad_key
            + jnp.einsum(
                "bhqk,bqhd->bkhd", grad_scores, query_block, preferred_element_type=jnp.float32
            )
            * factor
        )
    grad_query_rot = jnp.concatenate(grad_query_blocks, 1)
    grad_query = (
        rotate_back(grad_query_rot, cosine_table, sine_table)
        .astype(jnp.bfloat16)
        .reshape(rows_total, model_width)
    )
    grad_key_low = (
        rotate_back(grad_key, cosine_table, sine_table)
        .astype(jnp.bfloat16)
        .reshape(rows_total, model_width)
    )
    grad_value_low = grad_value.astype(jnp.bfloat16).reshape(rows_total, model_width)
    grad_w_query = rows_product(attn_in, grad_query)
    grad_w_key = rows_product(attn_in, grad_key_low)
    grad_w_value = rows_product(attn_in, grad_value_low)
    grad_attn_in = (
        right_transposed(grad_query, query_mat)
        + right_transposed(grad_key_low, key_mat)
        + right_transposed(grad_value_low, value_mat)
    )
    grad_gain_one = jnp.sum(grad_attn_in * normed_one, 0)
    grad_input = (grad_middle + norm_back(grad_attn_in * gain_first, normed_one, inv_one)).reshape(
        batch_size, length, model_width
    )
    replicas = lax.axis_size("rep")
    members = lax.axis_size("shard")
    parts = (
        lax.psum_scatter(grad_gain_one, "shard", scatter_dimension=0, tiled=True),
        lax.psum_scatter(grad_w_query, "shard", scatter_dimension=0, tiled=True),
        lax.psum_scatter(grad_w_key, "shard", scatter_dimension=0, tiled=True),
        lax.psum_scatter(grad_w_value, "shard", scatter_dimension=0, tiled=True),
        lax.psum_scatter(grad_w_out, "shard", scatter_dimension=0, tiled=True),
        lax.psum_scatter(grad_gain_two, "shard", scatter_dimension=0, tiled=True),
        lax.psum_scatter(grad_w_gate, "shard", scatter_dimension=0, tiled=True),
        lax.psum_scatter(grad_w_up, "shard", scatter_dimension=0, tiled=True),
        lax.psum_scatter(grad_w_down, "shard", scatter_dimension=0, tiled=True),
    )
    summed = (
        lax.psum(parts[0].astype(jnp.bfloat16), "rep").astype(jnp.float32),
        lax.psum(parts[1].astype(jnp.bfloat16), "rep").astype(jnp.float32),
        lax.psum(parts[2].astype(jnp.bfloat16), "rep").astype(jnp.float32),
        lax.psum(parts[3].astype(jnp.bfloat16), "rep").astype(jnp.float32),
        lax.psum(parts[4].astype(jnp.bfloat16), "rep").astype(jnp.float32),
        lax.psum(parts[5].astype(jnp.bfloat16), "rep").astype(jnp.float32),
        lax.psum(parts[6].astype(jnp.bfloat16), "rep").astype(jnp.float32),
        lax.psum(parts[7].astype(jnp.bfloat16), "rep").astype(jnp.float32),
        lax.psum(parts[8].astype(jnp.bfloat16), "rep").astype(jnp.float32),
    )
    inverse_count = 1.0 / (batch_size * replicas * members)
    return (
        output,
        grad_input,
        summed[0] * inverse_count,
        summed[1] * inverse_count,
        summed[2] * inverse_count,
        summed[3] * inverse_count,
        summed[4] * inverse_count,
        summed[5] * inverse_count,
        summed[6] * inverse_count,
        summed[7] * inverse_count,
        summed[8] * inverse_count,
    )


def solution(mesh):
    return jax.shard_map(
        per_device,
        mesh=mesh,
        in_specs=(
            P(("rep", "shard"), None, None),
            P(("rep", "shard"), None),
            P("shard"),
            P("shard", None),
            P("shard", None),
            P("shard", None),
            P("shard", None),
            P("shard"),
            P("shard", None),
            P("shard", None),
            P("shard", None),
            P(("rep", "shard"), None, None),
        ),
        out_specs=(
            P(("rep", "shard"), None, None),
            P(("rep", "shard"), None, None),
            P("shard"),
            P("shard", None),
            P("shard", None),
            P("shard", None),
            P("shard", None),
            P("shard"),
            P("shard", None),
            P("shard", None),
            P("shard", None),
        ),
        check_vma=False,
    )
```

profile of v0, /device:TPU:0, one launch (start us, length us, event | category | flops | bytes accessed | tf_op | source)
XLA Modules:
  0.0 944.5 jit_solution(17049137769246098057)
XLA Ops:
  15.7 35.2 %all-reduce.5 = (bf16[768]{0:T(1024)(128)(2,1)S(1)}, bf16[768]{0:T(1024)(128)(2,1)S(1)}) all-reduce(bf16[768]{0:T(1024)(128)(2,1)S(1)} %dynamic-update-slice, bf16[768]{0:T(1024)(128)(2,1)S(1)} %dynamic-update-slice.1), channel_id=1, replica_groups=mesh['rep'=2,'shard'=16] {'shard'}, use_global_device_ids=true, to_apply=%add | all-reduce | flops 1536 | bytes 6144
  54.4 2.6 copy.47
  60.4 30.6 %all-gather.12.cloned.1.call-done = bf16[768,768]{1,0:T(8,128)(2,1)} async-done(((bf16[48,768]{1,0:T(8,128)(2,1)}), bf16[768,768]{1,0:T(8,128)(2,1)}) %all-gather.12.cloned.1.call-update) | async-done | bytes 1179664 | tf_op jit(solution)/shard_map/all_gather | solution.py:105
  93.4 37.2 %all-gather.10.cloned.1.call-done = bf16[768,768]{1,0:T(8,128)(2,1)} async-done(((bf16[48,768]{1,0:T(8,128)(2,1)}), bf16[768,768]{1,0:T(8,128)(2,1)}) %all-gather.10.cloned.1.call-update) | async-done | bytes 1179664 | tf_op jit(solution)/shard_map/all_gather | solution.py:104
  133.0 4.0 convolution_convert_fusion
  141.4 11.3 %fusion.13 = (f32[12,512]{1,0:T(8,128)}, f32[12,512,1024]{2,1,0:T(8,128)}) fusion(pred[512,1024]{1,0:T(8,128)(4,1)S(1)} %get-tuple-element.66, bf16[1024,12,32]{0,2,1:T(8,128)(2,1)S(1)} %get-tuple-element.58, bf16[1024,12,32]{0,2,1:T(8,128)(2,1)S(1)} %get-tuple-element.57, bf16[1,1024,12,32]{1,3,2,0:T(8,128)(2,1)S(1)} %get-tuple-element.63, ...), kind=kOutput, calls=%fused_computation.23 | convolution fusion | flops 828893184 | bytes 28860416 | tf_op jit(solution)/shard_map/bqhd,bkhd->bhqk/dot_general | solution.py:76
  152.7 14.6 %fusion.12 = (f32[12,512]{1,0:T(8,128)}, f32[12,512,1024]{2,1,0:T(8,128)}) fusion(pred[512,1024]{1,0:T(8,128)(4,1)S(1)} %get-tuple-element.65, bf16[1024,12,32]{0,2,1:T(8,128)(2,1)} %copy-done.10, bf16[1024,12,32]{0,2,1:T(8,128)(2,1)} %copy-done.8, bf16[1,1024,12,32]{1,3,2,0:T(8,128)(2,1)} %copy-done.3, bf16[1,1024,12,32]{1,3,2,0:T(8,128)(2,1)} %copy-done.1), kind=kOutput, calls=%fused_computation.22 | convolution fusion | flops 828893184 | bytes 28860416 | tf_op jit(solution)/shard_map/bqhd,bkhd->bhqk/dot_general | solution.py:76
  167.3 12.8 %fusion.1 = f32[12,512]{1,0:T(8,128)S(1)} fusion(f32[12,512]{1,0:T(8,128)} %get-tuple-element.73, f32[12,512,1024]{2,1,0:T(8,128)} %get-tuple-element.74, pred[512,1024]{1,0:T(8,128)(4,1)S(1)} %get-tuple-element.66), kind=kLoop, calls=%fused_computation.13 | loop fusion | flops 25159680 | bytes 25739264 | tf_op jit(solution)/shard_map/reduce_sum | solution.py:135
  180.3 8.7 fusion.49
  188.9 13.4 %fusion = f32[12,512]{1,0:T(8,128)S(1)} fusion(f32[12,512]{1,0:T(8,128)} %get-tuple-element.75, f32[12,512,1024]{2,1,0:T(8,128)} %get-tuple-element.76, pred[512,1024]{1,0:T(8,128)(4,1)S(1)} %get-tuple-element.65), kind=kLoop, calls=%fused_computation.12 | loop fusion | flops 25159680 | bytes 25739264 | tf_op jit(solution)/shard_map/reduce_sum | solution.py:135
  204.9 9.2 fusion.48
  215.5 3.4 multiply_reduce_fusion.4
  222.1 9.1 fusion.97
  231.1 31.5 %all-gather.16.cloned.1.call-done = bf16[768,2048]{1,0:T(8,128)(2,1)} async-done(((bf16[48,2048]{1,0:T(8,128)(2,1)}), bf16[768,2048]{1,0:T(8,128)(2,1)}) %all-gather.16.cloned.1.call-update) | async-done | bytes 3145744 | tf_op jit(solution)/shard_map/all_gather | solution.py:109
  262.6 9.1 fusion.96
  271.7 37.2 %all-gather.20.cloned.1.call-done = bf16[2048,768]{1,0:T(8,128)(2,1)} async-done(((bf16[128,768]{1,0:T(8,128)(2,1)}), bf16[2048,768]{1,0:T(8,128)(2,1)}) %all-gather.20.cloned.1.call-update) | async-done | bytes 3145744 | tf_op jit(solution)/shard_map/all_gather | solution.py:111
  309.0 14.4 %multiply_convert_fusion.2 = (bf16[1024,2048]{1,0:T(8,128)(2,1)S(1)}, bf16[1024,2048]{1,0:T(8,128)(2,1)}, bf16[1024,2048]{1,0:T(8,128)(2,1)}) fusion(f32[1024,2048]{1,0:T(8,128)} %fusion.96, f32[1024,2048]{1,0:T(8,128)} %fusion.97, bf16[2048,768]{1,0:T(8,128)(2,1)} %all-gather.20.cloned.1.call-done, bf16[1,1024,768]{2,1,0:T(8,128)(2,1)} %param.23), kind=kOutput, calls=%fused_computation.24 | convolution fusion | flops 3254779904 | bytes 34078720 | tf_op jit(solution)/shard_map/dot_general | solution.py:64
  323.4 7.4 fusion.98
  330.8 4.6 multiply_reduce_fusion.2
  337.8 2.9 fusion.55
  340.8 3.6 convolution_convert_fusion.1
  344.5 12.4 %fusion.4 = f32[12,64,1024]{2,1,0:T(8,128)S(1)} fusion(f32[12,512]{1,0:T(8,128)S(1)} %log_add_fusion, f32[12,512,1024]{2,1,0:T(8,128)} %get-tuple-element.74, pred[512,1024]{1,0:T(8,128)(4,1)S(1)} %get-tuple-element.66, bf16[1,1024,12,64]{1,3,2,0:T(8,128)(2,1)S(1)} %bitcast.182), kind=kOutput, calls=%fused_computation.16 | convolution fusion | flops 830472192 | bytes 29655040 | tf_op jit(solution)/shard_map/bhqk,bqhd->bkhd/dot_general | solution.py:195
  357.0 11.8 %add_convert_fusion = bf16[12,64,1024]{2,1,0:T(8,128)(2,1)S(1)} fusion(f32[12,64,1024]{2,1,0:T(8,128)S(1)} %fusion.4, f32[12,512]{1,0:T(8,128)S(1)} %log_add_fusion.1, f32[12,512,1024]{2,1,0:T(8,128)} %get-tuple-element.76, pred[512,1024]{1,0:T(8,128)(4,1)S(1)} %get-tuple-element.65, bf16[1,1024,12,64]{1,3,2,0:T(8,128)(2,1)S(1)} %bitcast.183), kind=kOutput, calls=%fused_computation.50 | convolution fusion | flops 832045056 | bytes 31227904 | tf_op jit(solution)/shard_map/bhqk,bqhd->bkhd/dot_general | solution.py:195
  370.0 2.9 fusion.41
  372.9 18.2 %multiply_reduce_fusion = (f32[12,512]{1,0:T(8,128)S(1)}, f32[12,512,1024]{2,1,0:T(8,128)}) fusion(f32[12,512]{1,0:T(8,128)S(1)} %log_add_fusion, f32[12,512,1024]{2,1,0:T(8,128)} %get-tuple-element.74, pred[512,1024]{1,0:T(8,128)(4,1)S(1)} %get-tuple-element.66, bf16[1024,12,64]{0,2,1:T(8,128)(2,1)} %convolution_convert_fusion, ...), kind=kOutput, calls=%fused_computation.1 | convolution fusion | flops 836757504 | bytes 53264384 | tf_op jit(solution)/shard_map/bqhd,bkhd->bhqk/dot_general | solution.py:198
  391.1 18.2 %multiply_reduce_fusion.1 = (f32[12,512]{1,0:T(8,128)S(1)}, f32[12,512,1024]{2,1,0:T(8,128)}) fusion(f32[12,512]{1,0:T(8,128)S(1)} %log_add_fusion.1, f32[12,512,1024]{2,1,0:T(8,128)} %get-tuple-element.76, pred[512,1024]{1,0:T(8,128)(4,1)S(1)} %get-tuple-element.65, bf16[1024,12,64]{0,2,1:T(8,128)(2,1)} %convolution_convert_fusion, ...), kind=kOutput, calls=%fused_computation.4 | convolution fusion | flops 836757504 | bytes 53264384 | tf_op jit(solution)/shard_map/bqhd,bkhd->bhqk/dot_general | solution.py:198
  409.4 43.6 %multiply_convert_fusion = (bf16[12,512,1024]{2,1,0:T(8,128)(2,1)}, bf16[12,512,1024]{2,1,0:T(8,128)(2,1)}) fusion(f32[12,512,1024]{2,1,0:T(8,128)} %get-tuple-element.83, f32[12,512]{1,0:T(8,128)S(1)} %get-tuple-element.82, f32[12,512]{1,0:T(8,128)S(1)} %log_add_fusion, f32[12,512,1024]{2,1,0:T(8,128)} %get-tuple-element.74, ...), kind=kLoop, calls=%fused_computation | loop fusion | flops 75497472 | bytes 126976000 | tf_op jit(solution)/shard_map/convert_element_type | solution.py:203
  453.1 7.1 fusion.85
  460.1 9.7 %multiply_bitcast_fusion.2 = f32[1,512,12,64]{1,3,2,0:T(8,128)} fusion(bf16[12,512,1024]{2,1,0:T(8,128)(2,1)} %get-tuple-element.86, bf16[1024,12,32]{0,2,1:T(8,128)(2,1)S(1)} %copy-done.11, bf16[1024,12,32]{0,2,1:T(8,128)(2,1)S(1)} %copy-done.9), kind=kOutput, calls=%fused_computation.89 | convolution fusion | flops 808845312 | bytes 15728640 | tf_op jit(solution)/shard_map/bhqk,bkhd->bqhd/dot_general | solution.py:205
  469.8 9.7 %multiply_bitcast_fusion.1 = f32[1,512,12,64]{1,3,2,0:T(8,128)} fusion(bf16[12,512,1024]{2,1,0:T(8,128)(2,1)} %get-tuple-element.85, bf16[1024,12,32]{0,2,1:T(8,128)(2,1)S(1)} %copy-done.11, bf16[1024,12,32]{0,2,1:T(8,128)(2,1)S(1)} %copy-done.9), kind=kOutput, calls=%fused_computation.88 | convolution fusion | flops 808845312 | bytes 15728640 | tf_op jit(solution)/shard_map/bhqk,bkhd->bqhd/dot_general | solution.py:205
  479.6 7.1 multiply_bitcast_fusion
  489.3 2.9 fusion.43
  493.6 2.9 fusion.39
  496.6 8.9 fusion.100
  505.6 8.9 fusion.99
  514.6 8.8 fusion.32
  524.3 8.7 fusion.45
  535.6 3.3 fusion.101
  540.7 3.6 fusion.25
  544.3 31.8 %all-reduce.4 = (bf16[768]{0:T(1024)(128)(2,1)S(1)}, bf16[768]{0:T(1024)(128)(2,1)S(1)}) all-reduce(f32[768]{0:T(1024)S(1)} %get-tuple-element.35, f32[768]{0:T(1024)S(1)} %copy-done.42), channel_id=2, replica_groups=mesh['rep'=2,'shard'=16] {'shard'}, use_global_device_ids=true, to_apply=%region_11.12.clone | all-reduce | flops 1536 | bytes 9216
  581.0 39.4 %reduce-scatter.10.cloned.1.call-done = f32[48,768]{1,0:T(8,128)} async-done(((f32[768,768]{1,0:T(8,128)}), f32[48,768]{1,0:T(8,128)}) %reduce-scatter.10.cloned.1.call-update) | async-done | bytes 147472 | tf_op jit(solution)/shard_map/reduce_scatter | solution.py:244
  621.9 86.6 %reduce-scatter.18.cloned.1.call-done = f32[48,2048]{1,0:T(8,128)} async-done(((f32[768,2048]{1,0:T(8,128)}), f32[48,2048]{1,0:T(8,128)}) %reduce-scatter.18.cloned.1.call-update) | async-done | bytes 393232 | tf_op jit(solution)/shard_map/reduce_scatter | solution.py:249
  710.2 87.3 %reduce-scatter.16.cloned.1.call-done = f32[48,2048]{1,0:T(8,128)} async-done(((f32[768,2048]{1,0:T(8,128)}), f32[48,2048]{1,0:T(8,128)}) %reduce-scatter.16.cloned.1.call-update) | async-done | bytes 393232 | tf_op jit(solution)/shard_map/reduce_scatter | solution.py:248
  799.2 86.5 %reduce-scatter.20.cloned.1.call-done = f32[128,768]{1,0:T(8,128)} async-done(((f32[2048,768]{1,0:T(8,128)}), f32[128,768]{1,0:T(8,128)}) %reduce-scatter.20.cloned.1.call-update) | async-done | bytes 393232 | tf_op jit(solution)/shard_map/reduce_scatter | solution.py:250
  887.4 5.3 fusion.24
  892.7 3.7 copy.54
  896.4 5.0 all-reduce.6
  902.4 24.1 %all-reduce.10.cloned.1.call-done = (bf16[48,768]{1,0:T(8,128)(2,1)}, bf16[48,768]{1,0:T(8,128)(2,1)}, bf16[48,768]{1,0:T(8,128)(2,1)}, bf16[48,768]{1,0:T(8,128...) async-done(((bf16[48,768]{1,0:T(8,128)(2,1)}, bf16[48,768]{1,0:T(8,128)(2,1)}, bf16[48,768]{1,0:T(8,128)(2,1)}, ...) | async-done | bytes 884752 | tf_op jit(solution)/shard_map/psum | solution.py:254
  (195 shorter events, 66.8 us)
Async XLA Ops:
  7.2 50.8 %all-gather.8.cloned.1.call-start = ((), (), s32[]{:S(2)}) async-start(), calls=%async_computation.7 | async-start | bytes 1253376 | tf_op jit(solution)/shard_map/all_gather | solution.py:106
  7.9 83.1 %all-gather.12.cloned.1.call-start = ((), (), s32[]{:S(2)}) async-start(), calls=%async_computation.9 | async-start | bytes 1253376 | tf_op jit(solution)/shard_map/all_gather | solution.py:105
  8.7 122.0 %all-gather.10.cloned.1.call-start = ((), (), s32[]{:S(2)}) async-start(), calls=%async_computation.8 | async-start | bytes 1253376 | tf_op jit(solution)/shard_map/all_gather | solution.py:104
  9.4 206.1 %all-gather.14.cloned.1.call-start = ((), (), s32[]{:S(2)}) async-start(), calls=%async_computation.10 | async-start | bytes 1253376 | tf_op jit(solution)/shard_map/all_gather | solution.py:107
  10.0 212.1 %all-gather.18.cloned.1.call-start = ((), (), s32[]{:S(2)}) async-start(), calls=%async_computation.12 | async-start | bytes 3342336 | tf_op jit(solution)/shard_map/all_gather | solution.py:110
  10.6 252.1 %all-gather.16.cloned.1.call-start = ((), (), s32[]{:S(2)}) async-start(), calls=%async_computation.11 | async-start | bytes 3342336 | tf_op jit(solution)/shard_map/all_gather | solution.py:109
  11.1 297.8 %all-gather.20.cloned.1.call-start = ((), (), s32[]{:S(2)}) async-start(), calls=%async_computation.13 | async-start | bytes 3342336 | tf_op jit(solution)/shard_map/all_gather | solution.py:111
  11.9 564.4 %reduce-scatter.14.cloned.1.call-start = ((), (), s32[]{:S(2)}) async-start(), calls=%async_computation.17 | async-start | bytes 2506752 | tf_op jit(solution)/shard_map/reduce_scatter | solution.py:246
  50.9 87.7 %copy-start.37 = (f32[768]{0:T(1024)}, f32[768]{0:T(1024)S(1)}, u32[]{:S(2)}) copy-start(f32[768]{0:T(1024)S(1)} %convert_element_type.200) | copy-start | bytes 9220
  52.2 88.0 %copy-start.24 = (f32[1024,32]{0,1:T(8,128)}, f32[1024,32]{0,1:T(8,128)S(1)}, u32[]{:S(2)}) copy-start(f32[1024,32]{0,1:T(8,128)S(1)} %get-tuple-element.71) | copy-start | bytes 393220
  52.2 88.0 %copy-start.26 = (f32[1024,32]{0,1:T(8,128)}, f32[1024,32]{0,1:T(8,128)S(1)}, u32[]{:S(2)}) copy-start(f32[1024,32]{0,1:T(8,128)S(1)} %get-tuple-element.72) | copy-start | bytes 393220
  54.4 84.3 %copy-start.39 = (f32[1024]{0:T(1024)}, f32[1024]{0:T(1024)S(1)}, u32[]{:S(2)}) copy-start(f32[1024]{0:T(1024)S(1)} %add_rsqrt_fusion.1) | copy-start | bytes 12292
  141.4 11.3 %copy-start.1 = (bf16[1,1024,12,32]{1,3,2,0:T(8,128)(2,1)}, bf16[1,1024,12,32]{1,3,2,0:T(8,128)(2,1)S(1)}, u32[]{:S(2)}) copy-start(bf16[1,1024,12,32]{1,3,2,0:T(8,128)(2,1)S(1)} %get-tuple-element.63) | copy-start | bytes 2359300
  141.4 11.3 %copy-start.3 = (bf16[1,1024,12,32]{1,3,2,0:T(8,128)(2,1)}, bf16[1,1024,12,32]{1,3,2,0:T(8,128)(2,1)S(1)}, u32[]{:S(2)}) copy-start(bf16[1,1024,12,32]{1,3,2,0:T(8,128)(2,1)S(1)} %get-tuple-element.64) | copy-start | bytes 2359300
  141.4 11.3 %copy-start.8 = (bf16[1024,12,32]{0,2,1:T(8,128)(2,1)}, bf16[1024,12,32]{0,2,1:T(8,128)(2,1)S(1)}, u32[]{:S(2)}) copy-start(bf16[1024,12,32]{0,2,1:T(8,128)(2,1)S(1)} %get-tuple-element.57) | copy-start | bytes 2359300
  141.4 11.3 %copy-start.10 = (bf16[1024,12,32]{0,2,1:T(8,128)(2,1)}, bf16[1024,12,32]{0,2,1:T(8,128)(2,1)S(1)}, u32[]{:S(2)}) copy-start(bf16[1024,12,32]{0,2,1:T(8,128)(2,1)S(1)} %get-tuple-element.58) | copy-start | bytes 2359300
  152.7 27.5 %slice-start = ((s8[25165824]{0:T(1024)(128)(4,1)}), s8[4194304]{0:T(1024)(128)(4,1)S(1)}, s32[]{:S(2)}) async-start(s8[25165824]{0:T(1024)(128)(4,1)} %bitcast.171), calls=%async_computation.22 | async-start | bytes 8388608
  152.7 27.5 %slice-start.1 = ((s8[25165824]{0:T(1024)(128)(4,1)}), s8[4194304]{0:T(1024)(128)(4,1)S(1)}, s32[]{:S(2)}) async-start(s8[25165824]{0:T(1024)(128)(4,1)} %bitcast.171), calls=%async_computation.23 | async-start | bytes 8388608
  152.7 27.5 %slice-start.2 = ((s8[25165824]{0:T(1024)(128)(4,1)}), s8[4194304]{0:T(1024)(128)(4,1)S(1)}, s32[]{:S(2)}) async-start(s8[25165824]{0:T(1024)(128)(4,1)} %bitcast.171), calls=%async_computation.24 | async-start | bytes 8388608
  152.7 27.5 %slice-start.3 = ((s8[25165824]{0:T(1024)(128)(4,1)}), s8[4194304]{0:T(1024)(128)(4,1)S(1)}, s32[]{:S(2)}) async-start(s8[25165824]{0:T(1024)(128)(4,1)} %bitcast.171), calls=%async_computation.25 | async-start | bytes 8388608
  167.3 12.9 %slice-start.4 = ((s8[25165824]{0:T(1024)(128)(4,1)}), s8[4194304]{0:T(1024)(128)(4,1)S(1)}, s32[]{:S(2)}) async-start(s8[25165824]{0:T(1024)(128)(4,1)} %bitcast.171), calls=%async_computation.26 | async-start | bytes 8388608
  167.3 12.9 %slice-start.5 = ((s8[25165824]{0:T(1024)(128)(4,1)}), s8[4194304]{0:T(1024)(128)(4,1)S(1)}, s32[]{:S(2)}) async-start(s8[25165824]{0:T(1024)(128)(4,1)} %bitcast.171), calls=%async_computation.27 | async-start | bytes 8388608
  167.3 12.9 %copy-start.12 = (bf16[1024,12,64]{0,2,1:T(8,128)(2,1)S(1)}, bf16[1024,12,64]{0,2,1:T(8,128)(2,1)}, u32[]{:S(2)}) copy-start(bf16[1024,12,64]{0,2,1:T(8,128)(2,1)} %convolution_convert_fusion) | copy-start | bytes 4718596
  167.3 12.9 %copy-start.32 = (f32[12,512]{1,0:T(8,128)S(1)}, f32[12,512]{1,0:T(8,128)}, u32[]{:S(2)}) copy-start(f32[12,512]{1,0:T(8,128)} %get-tuple-element.73) | copy-start | bytes 73732
  180.3 8.7 copy-start.35
  188.9 15.9 %copy-start = (f32[12,512,1024]{2,1,0:T(8,128)S(1)}, f32[12,512,1024]{2,1,0:T(8,128)}, u32[]{:S(2)}) copy-start(f32[12,512,1024]{2,1,0:T(8,128)} %get-tuple-element.76) | copy-start | bytes 75497472
  188.9 15.9 %copy-start.34 = (f32[12,512]{1,0:T(8,128)S(1)}, f32[12,512]{1,0:T(8,128)}, u32[]{:S(2)}) copy-start(f32[12,512]{1,0:T(8,128)} %get-tuple-element.75) | copy-start | bytes 73732
  204.9 9.2 copy-start.31
  308.9 14.4 %copy-start.44 = (bf16[768,2048]{1,0:T(8,128)(2,1)S(1)}, bf16[768,2048]{1,0:T(8,128)(2,1)}, u32[]{:S(2)}) copy-start(bf16[768,2048]{1,0:T(8,128)(2,1)} %all-gather.16.cloned.1.call-done) | copy-start | bytes 9437188
  323.4 7.4 copy-start.45
  323.4 7.4 copy-start.6
  323.4 7.4 copy-start.43
  340.8 237.1 %reduce-scatter.12.cloned.1.call-start = ((), (), s32[]{:S(2)}) async-start(), calls=%async_computation.16 | async-start | bytes 2506752 | tf_op jit(solution)/shard_map/reduce_scatter | solution.py:245
  344.5 12.4 %copy-start.23 = (bf16[1024,768]{0,1:T(8,128)(2,1)}, bf16[1024,768]{0,1:T(8,128)(2,1)S(1)}, u32[]{:S(2)}) copy-start(bf16[1024,768]{0,1:T(8,128)(2,1)S(1)} %convolution_convert_fusion.1) | copy-start | bytes 4718596
  356.9 13.1 %copy-start.38 = (f32[768]{0:T(1024)S(1)}, f32[768]{0:T(1024)}, u32[]{:S(2)}) copy-start(f32[768]{0:T(1024)} %copy-done.37) | copy-start | bytes 9220
  356.9 13.1 %copy-start.40 = (f32[1024]{0:T(1024)S(1)}, f32[1024]{0:T(1024)}, u32[]{:S(2)}) copy-start(f32[1024]{0:T(1024)} %copy-done.39) | copy-start | bytes 12292
  409.3 170.1 %reduce-scatter.8.cloned.1.call-start = ((), (), s32[]{:S(2)}) async-start(), calls=%async_computation.14 | async-start | bytes 2506752 | tf_op jit(solution)/shard_map/reduce_scatter | solution.py:243
  409.4 43.6 %copy-start.2 = (bf16[1,1024,12,32]{1,3,2,0:T(8,128)(2,1)S(1)}, bf16[1,1024,12,32]{1,3,2,0:T(8,128)(2,1)}, u32[]{:S(2)}) copy-start(bf16[1,1024,12,32]{1,3,2,0:T(8,128)(2,1)} %copy-done.1) | copy-start | bytes 2359300
  409.4 43.6 %copy-start.4 = (bf16[1,1024,12,32]{1,3,2,0:T(8,128)(2,1)S(1)}, bf16[1,1024,12,32]{1,3,2,0:T(8,128)(2,1)}, u32[]{:S(2)}) copy-start(bf16[1,1024,12,32]{1,3,2,0:T(8,128)(2,1)} %copy-done.3) | copy-start | bytes 2359300
  479.5 7.2 copy-start.14
  479.5 7.2 copy-start.15
  479.5 7.2 copy-start.25
  479.6 7.2 copy-start.27
  492.3 128.1 %reduce-scatter.10.cloned.1.call-start = ((), (), s32[]{:S(2)}) async-start(), calls=%async_computation.15 | async-start | bytes 2506752 | tf_op jit(solution)/shard_map/reduce_scatter | solution.py:244
  496.6 211.9 %reduce-scatter.18.cloned.1.call-start = ((), (), s32[]{:S(2)}) async-start(), calls=%async_computation.19 | async-start | bytes 6684672 | tf_op jit(solution)/shard_map/reduce_scatter | solution.py:249
  505.6 291.9 %reduce-scatter.16.cloned.1.call-start = ((), (), s32[]{:S(2)}) async-start(), calls=%async_computation.18 | async-start | bytes 6684672 | tf_op jit(solution)/shard_map/reduce_scatter | solution.py:248
  514.6 371.1 %reduce-scatter.20.cloned.1.call-start = ((), (), s32[]{:S(2)}) async-start(), calls=%async_computation.20 | async-start | bytes 6684672 | tf_op jit(solution)/shard_map/reduce_scatter | solution.py:250
  523.4 403.0 %all-reduce.10.cloned.1.call-start = ((), (), s32[]{:S(2)}) async-start(), calls=%async_computation.21 | async-start | bytes 1769472 | tf_op jit(solution)/shard_map/psum | solution.py:254
  (19 other events, 56.9 us)
Sparse Core Ops, SparseCore 0:
  10.3 41.1 all-gather.7
  53.7 37.2 all-gather.11
  93.3 37.2 all-gather.9
  132.8 37.3 all-gather.13
  172.3 44.1 all-gather.17
  218.6 43.9 all-gather.15
  264.9 43.9 all-gather.19
  340.9 61.7 reduce-scatter.13
  409.4 61.8 reduce-scatter.11
  492.4 61.8 reduce-scatter.7
  558.5 61.8 reduce-scatter.9
  624.2 84.2 reduce-scatter.17
  713.0 84.4 reduce-scatter.15
  801.3 84.3 reduce-scatter.19
  889.6 36.7 all-reduce.9
where the time goes:
time: 954 us; the launch traced here: 945 us
  waiting for transfers between devices  465 us (49%)
  matrix products  252 us (26%)
  other arithmetic  107 us (11%)
  blocking collectives  72 us (8%)
  local copies, waits for them, and re-layouts  31.4 us (3%)
  between operations  16.3 us (2%)
    reduce_scatter x1, waiting for transfers between devices, per_device(): lax.psum_scatter(grad_w_gate, 'shard', scatter_dimension=0, tiled=True)  87.3 us
    reduce_scatter x1, waiting for transfers between devices, per_device(): lax.psum_scatter(grad_w_up, 'shard', scatter_dimension=0, tiled=True)  86.6 us
    reduce_scatter x1, waiting for transfers between devices, per_device(): lax.psum_scatter(grad_w_down, 'shard', scatter_dimension=0, tiled=True)  86.5 us
    unnamed x2, blocking collectives  67.1 us
    convert_element_type x1, other arithmetic, per_device(): grad_scores = (probs_full * (grad_probs - jnp.sum(probs_full * grad_probs...  43.6 us
    reduce_scatter x1, waiting for transfers between devices, per_device(): lax.psum_scatter(grad_w_key, 'shard', scatter_dimension=0, tiled=True)  39.4 us
    dot_general x7, matrix products, right_transposed(): lax.dot_general(left, right, (((1,), (1,)), ((), ())), preferred_element_...  38.3 us
    dot_general x7, matrix products, rows_product(): lax.dot_general(left, right, (((0,), (0,)), ((), ())), preferred_element_...  38.2 us
  transfers between devices with their start and end apart: 15, of which 9 were waited for; matrix products, arithmetic and copies ran while one was open for 36% of the time, Pallas kernels for 0%

commit v1 on v0

--- a/solution.py
+++ b/solution.py
@@ -9,6 +9,28 @@
 epsilon = 1e-06
 rope_base = 10000.0
 masked_score = -1e30
+
+
+def in_order(parts, dim):
+    lengths = list(parts.shape[1:])
+    lengths[dim] *= parts.shape[0]
+    return jnp.moveaxis(parts, 0, dim).reshape(lengths)
+
+
+def collect(x, axis, dim):
+    count = lax.axis_size(axis)
+    pairs = [(i, (i + 1) % count) for i in range(count)]
+    back = [(b, a) for a, b in pairs]
+    lower, upper = ([], [])
+    for step in range(count - 1):
+        if step % 2 == 0:
+            lower.append(lax.ppermute(lower[-1] if lower else x, axis, pairs))
+        else:
+            upper.append(lax.ppermute(upper[-1] if upper else x, axis, back))
+    blocks = jnp.stack([*lower[::-1], x, *upper])
+    shift = lax.axis_index(axis) - len(lower)
+    blocks = blocks[(jnp.arange(count) - shift) % count]
+    return in_order(blocks, dim)
 
 
 def rope_tables(length, head_size):
@@ -102,7 +124,7 @@
     gain_one, query_mat, key_mat, value_mat, out_mat, gain_two, gate_mat, up_mat, down_mat = (
         lax.all_gather(attn_gain, "shard", axis=0, tiled=True),
         lax.all_gather(w_query, "shard", axis=0, tiled=True),
-        lax.all_gather(w_key, "shard", axis=0, tiled=True),
+        collect(w_key, "shard", 0),
         lax.all_gather(w_value, "shard", axis=0, tiled=True),
         lax.all_gather(w_out, "shard", axis=0, tiled=True),
         lax.all_gather(ffn_gain, "shard", axis=0, tiled=True),

time: 954 us -> 925 us (0.970)
  waiting for transfers between devices: 465 us -> 395 us
  starting transfers between devices: 0.81 us -> 30 us
  local copies, waits for them, and re-layouts: 31.4 us -> 47.5 us
    all_gather x1, waiting for transfers between devices: 37.2 us -> 0.01 us  [per_device(): lax.all_gather(w_query, 'shard', axis=0, tiled=True)]
    all_gather x1, waiting for transfers between devices: 30.6 us -> 0.01 us  [per_device(): lax.all_gather(w_key, 'shard', axis=0, tiled=True)]
    ppermute x0 -> x15, starting transfers between devices: none -> 29.3 us  [the longest x7 28.2 us: collect(): upper.append(lax.ppermute(upper[-1] if upper else x, axis, back))]
    all_gather x1, waiting for transfers between devices: 31.5 us -> 4.06 us  [per_device(): lax.all_gather(w_gate, 'shard', axis=0, tiled=True)]
    ppermute x0 -> x15, waiting for transfers between devices: none -> 14.7 us  [the longest x8 8.77 us: collect(): lower.append(lax.ppermute(lower[-1] if lower else x, axis, pairs))]
    unnamed x115 -> x122, local copies, waits for them, and re-layouts: 23.6 us -> 36.1 us
    reduce_scatter x1, waiting for transfers between devices: 39.4 us -> 51.2 us  [per_device(): lax.psum_scatter(grad_w_key, 'shard', scatter_dimension=0, tiled=True)]
  transfers between devices with their start and end apart: 15 -> 30, of which waited for: 9 -> 13; matrix products, arithmetic and copies ran while one was open for 36% -> 41% of each run, Pallas kernels for 0% -> 0%
where the time goes in v1:
time: 925 us; the launch traced here: 919 us
  waiting for transfers between devices  395 us (43%)
  matrix products  252 us (27%)
  other arithmetic  108 us (12%)
  blocking collectives  71.1 us (8%)
  local copies, waits for them, and re-layouts  47.5 us (5%)
  starting transfers between devices  30 us (3%)
  between operations  16.1 us (2%)
    reduce_scatter x1, waiting for transfers between devices, per_device(): lax.psum_scatter(grad_w_gate, 'shard', scatter_dimension=0, tiled=True)  87.4 us
    reduce_scatter x1, waiting for transfers between devices, per_device(): lax.psum_scatter(grad_w_up, 'shard', scatter_dimension=0, tiled=True)  86.5 us
    reduce_scatter x1, waiting for transfers between devices, per_device(): lax.psum_scatter(grad_w_down, 'shard', scatter_dimension=0, tiled=True)  86.5 us
    unnamed x2, blocking collectives  66.1 us
    reduce_scatter x1, waiting for transfers between devices, per_device(): lax.psum_scatter(grad_w_key, 'shard', scatter_dimension=0, tiled=True)  51.2 us
    convert_element_type x1, other arithmetic, per_device(): grad_scores = (probs_full * (grad_probs - jnp.sum(probs_full * grad_probs...  42.8 us
    dot_general x7, matrix products, right_transposed(): lax.dot_general(left, right, (((1,), (1,)), ((), ())), preferred_element_...  38.9 us
    dot_general x7, matrix products, rows_product(): lax.dot_general(left, right, (((0,), (0,)), ((), ())), preferred_element_...  37.4 us
  transfers between devices with their start and end apart: 30, of which 13 were waited for; matrix products, arithmetic and copies ran while one was open for 41% of the time, Pallas kernels for 0%

profile of v1, /device:TPU:0, one launch (start us, length us, event | category | flops | bytes accessed | tf_op | source)
XLA Modules:
  0.0 919.3 jit_solution(17358592879348087035)
XLA Ops:
  11.7 5.1 collective-permute-start.8
  20.8 4.9 collective-permute-done.1
  25.7 4.5 collective-permute-start.9
  35.5 4.5 collective-permute-start.10
  42.4 4.6 collective-permute-start.11
  48.7 34.0 %all-reduce.5 = (bf16[768]{0:T(1024)(128)(2,1)S(1)}, bf16[768]{0:T(1024)(128)(2,1)S(1)}) all-reduce(bf16[768]{0:T(1024)(128)(2,1)S(1)} %dynamic-update-slice, bf16[768]{0:T(1024)(128)(2,1)S(1)} %dynamic-update-slice.1), channel_id=1, replica_groups=mesh['rep'=2,'shard'=16] {'shard'}, use_global_device_ids=true, to_apply=%add | all-reduce | flops 1536 | bytes 6144
  88.0 4.6 collective-permute-start.13
  94.5 5.0 collective-permute-start.14
  115.9 4.4 convolution_bitcast_fusion
  125.1 4.0 convolution_convert_fusion
  132.2 10.8 %fusion.13 = (f32[12,512]{1,0:T(8,128)S(1)}, f32[12,512,1024]{2,1,0:T(8,128)}) fusion(pred[512,1024]{1,0:T(8,128)(4,1)S(1)} %get-tuple-element.66, bf16[1024,12,32]{0,2,1:T(8,128)(2,1)S(1)} %get-tuple-element.58, bf16[1024,12,32]{0,2,1:T(8,128)(2,1)S(1)} %get-tuple-element.57, bf16[1,1024,12,32]{1,3,2,0:T(8,128)(2,1)S(1)} %get-tuple-element.63, ...), kind=kOutput, calls=%fused_computation.24 | convolution fusion | flops 828893184 | bytes 28860416 | tf_op jit(solution)/shard_map/bqhd,bkhd->bhqk/dot_general | solution.py:98
  142.9 12.4 %fusion.1 = f32[12,512]{1,0:T(8,128)S(1)} fusion(f32[12,512]{1,0:T(8,128)S(1)} %get-tuple-element.73, f32[12,512,1024]{2,1,0:T(8,128)} %get-tuple-element.74, pred[512,1024]{1,0:T(8,128)(4,1)S(1)} %get-tuple-element.66), kind=kLoop, calls=%fused_computation.14 | loop fusion | flops 25159680 | bytes 25739264 | tf_op jit(solution)/shard_map/reduce_sum | solution.py:157
  158.4 9.6 %fusion.49 = bf16[1,512,12,64]{1,3,2,0:T(8,128)(2,1)} fusion(bf16[1024,12,64]{0,2,1:T(8,128)(2,1)} %convolution_convert_fusion, f32[12,512]{1,0:T(8,128)S(1)} %fusion.1, f32[12,512]{1,0:T(8,128)S(1)} %get-tuple-element.73, f32[12,512,1024]{2,1,0:T(8,128)S(1)} %copy-done, pred[512,1024]{1,0:T(8,128)(4,1)S(1)} %get-tuple-element.66), kind=kOutput, calls=%fused_computation.99 | convolution fusion | flops 837156864 | bytes 28098560 | tf_op jit(solution)/shard_map/bhqk,bkhd->bqhd/dot_general | solution.py:161
  168.0 12.1 %fusion.12 = (f32[12,512]{1,0:T(8,128)S(1)}, f32[12,512,1024]{2,1,0:T(8,128)}) fusion(pred[512,1024]{1,0:T(8,128)(4,1)S(1)} %get-tuple-element.65, bf16[1024,12,32]{0,2,1:T(8,128)(2,1)} %copy-done.11, bf16[1024,12,32]{0,2,1:T(8,128)(2,1)S(1)} %get-tuple-element.57, bf16[1,1024,12,32]{1,3,2,0:T(8,128)(2,1)S(1)} %get-tuple-element.64, ...), kind=kOutput, calls=%fused_computation.23 | convolution fusion | flops 828893184 | bytes 28860416 | tf_op jit(solution)/shard_map/bqhd,bkhd->bhqk/dot_general | solution.py:98
  180.2 12.4 %fusion = f32[12,512]{1,0:T(8,128)S(1)} fusion(f32[12,512]{1,0:T(8,128)S(1)} %get-tuple-element.75, f32[12,512,1024]{2,1,0:T(8,128)} %get-tuple-element.76, pred[512,1024]{1,0:T(8,128)(4,1)S(1)} %get-tuple-element.65), kind=kLoop, calls=%fused_computation.13 | loop fusion | flops 25159680 | bytes 25739264 | tf_op jit(solution)/shard_map/reduce_sum | solution.py:157
  195.8 9.0 fusion.48
  206.2 3.6 multiply_reduce_fusion.4
  213.0 9.1 fusion.99
  222.1 4.1 all-gather.14.cloned.1.call-done
  226.1 9.1 fusion.98
  235.2 37.1 %all-gather.18.cloned.1.call-done = bf16[2048,768]{1,0:T(8,128)(2,1)} async-done(((bf16[128,768]{1,0:T(8,128)(2,1)}), bf16[2048,768]{1,0:T(8,128)(2,1)}) %all-gather.18.cloned.1.call-update) | async-done | bytes 3145744 | tf_op jit(solution)/shard_map/all_gather | solution.py:133
  272.3 14.4 %multiply_convert_fusion.2 = (bf16[1024,2048]{1,0:T(8,128)(2,1)S(1)}, bf16[1024,2048]{1,0:T(8,128)(2,1)}, bf16[1024,2048]{1,0:T(8,128)(2,1)}) fusion(f32[1024,2048]{1,0:T(8,128)} %fusion.98, f32[1024,2048]{1,0:T(8,128)} %fusion.99, bf16[2048,768]{1,0:T(8,128)(2,1)} %all-gather.18.cloned.1.call-done, bf16[1,1024,768]{2,1,0:T(8,128)(2,1)} %param.23), kind=kOutput, calls=%fused_computation.25 | convolution fusion | flops 3254779904 | bytes 34078720 | tf_op jit(solution)/shard_map/dot_general | solution.py:86
  286.7 7.4 fusion.100
  294.2 4.6 multiply_reduce_fusion.2
  301.7 11.9 %fusion.4 = f32[12,64,1024]{2,1,0:T(8,128)S(1)} fusion(f32[12,512]{1,0:T(8,128)S(1)} %copy-done.34, f32[12,512,1024]{2,1,0:T(8,128)} %get-tuple-element.74, pred[512,1024]{1,0:T(8,128)(4,1)S(1)} %get-tuple-element.66, bf16[1,1024,12,64]{1,3,2,0:T(8,128)(2,1)S(1)} %bitcast.217), kind=kOutput, calls=%fused_computation.17 | convolution fusion | flops 830472192 | bytes 29655040 | tf_op jit(solution)/shard_map/bhqk,bqhd->bkhd/dot_general | solution.py:217
  313.7 11.9 %add_convert_fusion = bf16[12,64,1024]{2,1,0:T(8,128)(2,1)S(1)} fusion(f32[12,64,1024]{2,1,0:T(8,128)S(1)} %fusion.4, f32[12,512]{1,0:T(8,128)S(1)} %log_add_fusion.1, f32[12,512,1024]{2,1,0:T(8,128)} %get-tuple-element.76, pred[512,1024]{1,0:T(8,128)(4,1)S(1)} %get-tuple-element.65, bf16[1,1024,12,64]{1,3,2,0:T(8,128)(2,1)S(1)} %bitcast.218), kind=kOutput, calls=%fused_computation.51 | convolution fusion | flops 832045056 | bytes 31227904 | tf_op jit(solution)/shard_map/bhqk,bqhd->bkhd/dot_general | solution.py:217
  329.7 5.2 fusion.55
  334.9 18.3 %multiply_reduce_fusion = (f32[12,512]{1,0:T(8,128)S(1)}, f32[12,512,1024]{2,1,0:T(8,128)}) fusion(f32[12,512]{1,0:T(8,128)S(1)} %copy-done.34, f32[12,512,1024]{2,1,0:T(8,128)} %get-tuple-element.74, pred[512,1024]{1,0:T(8,128)(4,1)S(1)} %get-tuple-element.66, bf16[1024,12,64]{0,2,1:T(8,128)(2,1)} %convolution_convert_fusion, ...), kind=kOutput, calls=%fused_computation.2 | convolution fusion | flops 836757504 | bytes 53264384 | tf_op jit(solution)/shard_map/bqhd,bkhd->bhqk/dot_general | solution.py:220
  353.2 18.2 %multiply_reduce_fusion.1 = (f32[12,512]{1,0:T(8,128)S(1)}, f32[12,512,1024]{2,1,0:T(8,128)}) fusion(f32[12,512]{1,0:T(8,128)S(1)} %log_add_fusion.1, f32[12,512,1024]{2,1,0:T(8,128)} %get-tuple-element.76, pred[512,1024]{1,0:T(8,128)(4,1)S(1)} %get-tuple-element.65, bf16[1024,12,64]{0,2,1:T(8,128)(2,1)} %convolution_convert_fusion, ...), kind=kOutput, calls=%fused_computation.5 | convolution fusion | flops 836757504 | bytes 53264384 | tf_op jit(solution)/shard_map/bqhd,bkhd->bhqk/dot_general | solution.py:220
  371.6 42.8 %multiply_convert_fusion = (bf16[12,512,1024]{2,1,0:T(8,128)(2,1)}, bf16[12,512,1024]{2,1,0:T(8,128)(2,1)}) fusion(f32[12,512,1024]{2,1,0:T(8,128)} %get-tuple-element.83, f32[12,512]{1,0:T(8,128)S(1)} %get-tuple-element.82, f32[12,512]{1,0:T(8,128)S(1)} %copy-done.34, f32[12,512,1024]{2,1,0:T(8,128)} %get-tuple-element.74, ...), kind=kLoop, calls=%fused_computation.1 | loop fusion | flops 75497472 | bytes 126976000 | tf_op jit(solution)/shard_map/convert_element_type | solution.py:225
  414.4 7.4 fusion.87
  421.8 8.5 multiply_bitcast_fusion.2
  430.3 9.7 %multiply_bitcast_fusion.1 = f32[1,512,12,64]{1,3,2,0:T(8,128)} fusion(bf16[12,512,1024]{2,1,0:T(8,128)(2,1)} %get-tuple-element.85, bf16[1024,12,32]{0,2,1:T(8,128)(2,1)S(1)} %copy-done.12, bf16[1024,12,32]{0,2,1:T(8,128)(2,1)S(1)} %copy-done.10), kind=kOutput, calls=%fused_computation.89 | convolution fusion | flops 808845312 | bytes 15728640 | tf_op jit(solution)/shard_map/bhqk,bkhd->bqhd/dot_general | solution.py:227
  439.9 7.2 multiply_bitcast_fusion
  458.1 7.5 fusion.102
  465.7 7.5 fusion.101
  474.7 8.4 fusion.32
  484.0 8.9 fusion.45
  495.7 4.3 fusion.103
  507.1 32.1 %all-reduce.4 = (bf16[768]{0:T(1024)(128)(2,1)S(1)}, bf16[768]{0:T(1024)(128)(2,1)S(1)}) all-reduce(f32[768]{0:T(1024)S(1)} %get-tuple-element.35, f32[768]{0:T(1024)S(1)} %copy-done.40), channel_id=2, replica_groups=mesh['rep'=2,'shard'=16] {'shard'}, use_global_device_ids=true, to_apply=%region_11.12.clone | all-reduce | flops 1536 | bytes 9216
  544.0 51.2 %reduce-scatter.10.cloned.1.call-done = f32[48,768]{1,0:T(8,128)} async-done(((f32[768,768]{1,0:T(8,128)}), f32[48,768]{1,0:T(8,128)}) %reduce-scatter.10.cloned.1.call-update) | async-done | bytes 147472 | tf_op jit(solution)/shard_map/reduce_scatter | solution.py:266
  596.8 86.5 %reduce-scatter.18.cloned.1.call-done = f32[48,2048]{1,0:T(8,128)} async-done(((f32[768,2048]{1,0:T(8,128)}), f32[48,2048]{1,0:T(8,128)}) %reduce-scatter.18.cloned.1.call-update) | async-done | bytes 393232 | tf_op jit(solution)/shard_map/reduce_scatter | solution.py:271
  685.0 87.4 %reduce-scatter.16.cloned.1.call-done = f32[48,2048]{1,0:T(8,128)} async-done(((f32[768,2048]{1,0:T(8,128)}), f32[48,2048]{1,0:T(8,128)}) %reduce-scatter.16.cloned.1.call-update) | async-done | bytes 393232 | tf_op jit(solution)/shard_map/reduce_scatter | solution.py:270
  774.1 86.5 %reduce-scatter.20.cloned.1.call-done = f32[128,768]{1,0:T(8,128)} async-done(((f32[2048,768]{1,0:T(8,128)}), f32[128,768]{1,0:T(8,128)}) %reduce-scatter.20.cloned.1.call-update) | async-done | bytes 393232 | tf_op jit(solution)/shard_map/reduce_scatter | solution.py:272
  862.3 5.2 fusion.24
  867.5 3.7 copy.54
  871.2 5.0 all-reduce.6
  877.2 24.1 %all-reduce.10.cloned.1.call-done = (bf16[48,768]{1,0:T(8,128)(2,1)}, bf16[48,768]{1,0:T(8,128)(2,1)}, bf16[48,768]{1,0:T(8,128)(2,1)}, bf16[48,768]{1,0:T(8,128...) async-done(((bf16[48,768]{1,0:T(8,128)(2,1)}, bf16[48,768]{1,0:T(8,128)(2,1)}, bf16[48,768]{1,0:T(8,128)(2,1)}, ...) | async-done | bytes 884752 | tf_op jit(solution)/shard_map/psum | solution.py:276
  (235 shorter events, 112.7 us)
Async XLA Ops:
  7.2 113.2 %all-gather.8.cloned.1.call-start = ((), (), s32[]{:S(2)}) async-start(), calls=%async_computation.7 | async-start | bytes 1253376 | tf_op jit(solution)/shard_map/all_gather | solution.py:128
  7.9 114.8 %all-gather.10.cloned.1.call-start = ((), (), s32[]{:S(2)}) async-start(), calls=%async_computation.8 | async-start | bytes 1253376 | tf_op jit(solution)/shard_map/all_gather | solution.py:126
  8.7 197.6 %all-gather.12.cloned.1.call-start = ((), (), s32[]{:S(2)}) async-start(), calls=%async_computation.9 | async-start | bytes 1253376 | tf_op jit(solution)/shard_map/all_gather | solution.py:129
  9.4 203.6 %all-gather.16.cloned.1.call-start = ((), (), s32[]{:S(2)}) async-start(), calls=%async_computation.11 | async-start | bytes 3342336 | tf_op jit(solution)/shard_map/all_gather | solution.py:132
  10.0 216.2 %all-gather.14.cloned.1.call-start = ((), (), s32[]{:S(2)}) async-start(), calls=%async_computation.10 | async-start | bytes 3342336 | tf_op jit(solution)/shard_map/all_gather | solution.py:131
  10.6 261.7 %all-gather.18.cloned.1.call-start = ((), (), s32[]{:S(2)}) async-start(), calls=%async_computation.12 | async-start | bytes 3342336 | tf_op jit(solution)/shard_map/all_gather | solution.py:133
  11.1 35.9 %copy-start.41 = (u32[32]{0:T(128)S(1)}, u32[32]{0:T(128)}, u32[]{:S(2)}) copy-start(u32[32]{0:T(128)} %constant.104) | copy-start | bytes 388
  11.1 37.1 %copy-start.45 = (bf16[48]{0:T(256)(128)(2,1)S(1)}, bf16[48]{0:T(256)(128)(2,1)}, u32[]{:S(2)}) copy-start(bf16[48]{0:T(256)(128)(2,1)} %param.14) | copy-start | bytes 292
  11.2 37.4 %copy-start.46 = (bf16[48]{0:T(256)(128)(2,1)S(1)}, bf16[48]{0:T(256)(128)(2,1)}, u32[]{:S(2)}) copy-start(bf16[48]{0:T(256)(128)(2,1)} %param.19) | copy-start | bytes 292
  11.2 488.8 %all-gather.20.cloned.1.call-start = ((), (), s32[]{:S(2)}) async-start(), calls=%async_computation.13 | async-start | bytes 1253376 | tf_op jit(solution)/shard_map/all_gather | solution.py:180
  11.2 7.9 collective-permute-start
  11.7 14.0 %collective-permute-start.8 = (bf16[48,768]{1,0:T(8,128)(2,1)}, bf16[48,768]{1,0:T(8,128)(2,1)S(1)}, u32[]{:S(2)}, u32[]{:S(2)}) collective-permute-start(bf16[48,768]{1,0:T(8,128)(2,1)} %param.16), channel_id=1, source_target_pairs={{1,0},{2,1},{3,2},{4,3},{5,4},{6,5},{7,6},{8,7},{9,8},{10,9},{11,1... | collective-permute-start | bytes 221192 | tf_op jit(solution)/shard_map/ppermute | solution.py:29
  16.8 522.6 %reduce-scatter.14.cloned.1.call-start = ((), (), s32[]{:S(2)}) async-start(), calls=%async_computation.17 | async-start | bytes 2506752 | tf_op jit(solution)/shard_map/reduce_scatter | solution.py:268
  19.1 6.6 collective-permute-start.1
  25.7 6.9 collective-permute-start.2
  25.7 9.8 %collective-permute-start.9 = (bf16[48,768]{1,0:T(8,128)(2,1)S(1)}, bf16[48,768]{1,0:T(8,128)(2,1)S(1)}, u32[]{:S(2)}, u32[]{:S(2)}) collective-permute-start(bf16[48,768]{1,0:T(8,128)(2,1)S(1)} %collective-permute-done.8), channel_id=1, source_target_pairs={{1,0},{2,1},{3,2},{4,3},{5,4},{6,5},{7,6},{8,7},{9,8},{10,9},{11,1... | collective-permute-start | bytes 221192 | tf_op jit(solution)/shard_map/ppermute | solution.py:29
  32.5 7.5 collective-permute-start.3
  33.7 96.9 %copy-start.28 = (f32[1024,32]{0,1:T(8,128)}, f32[1024,32]{0,1:T(8,128)S(1)}, u32[]{:S(2)}) copy-start(f32[1024,32]{0,1:T(8,128)S(1)} %get-tuple-element.71) | copy-start | bytes 393220
  35.5 70.0 %copy-start.35 = (bf16[48,768]{1,0:T(8,128)(2,1)S(1)}, bf16[48,768]{1,0:T(8,128)(2,1)}, u32[]{:S(2)}) copy-start(bf16[48,768]{1,0:T(8,128)(2,1)} %param.16) | copy-start | bytes 221188
  35.5 6.8 collective-permute-start.10
  40.0 6.9 collective-permute-start.4
  42.4 43.0 %collective-permute-start.11 = (bf16[48,768]{1,0:T(8,128)(2,1)S(1)}, bf16[48,768]{1,0:T(8,128)(2,1)S(1)}, u32[]{:S(2)}, u32[]{:S(2)}) collective-permute-start(bf16[48,768]{1,0:T(8,128)(2,1)S(1)} %collective-permute-done.10), channel_id=1, source_target_pairs={{1,0},{2,1},{3,2},{4,3},{5,4},{6,5},{7,6},{8,7},{9,8},{10,9},{11,1... | collective-permute-start | bytes 221192 | tf_op jit(solution)/shard_map/ppermute | solution.py:29
  47.0 38.4 %collective-permute-start.5 = (bf16[48,768]{1,0:T(8,128)(2,1)S(1)}, bf16[48,768]{1,0:T(8,128)(2,1)}, u32[]{:S(2)}, u32[]{:S(2)}) collective-permute-start(bf16[48,768]{1,0:T(8,128)(2,1)S(1)} %collective-permute-done.4), channel_id=1, source_target_pairs={{0,1},{1,2},{2,3},{3,4},{4,5},{5,6},{6,7},{7,8},{8,9},{9,10},{10,1... | collective-permute-start | bytes 221192 | tf_op jit(solution)/shard_map/ppermute | solution.py:27
  47.0 82.1 %copy-start.36 = (f32[1024]{0:T(1024)}, f32[1024]{0:T(1024)S(1)}, u32[]{:S(2)}) copy-start(f32[1024]{0:T(1024)S(1)} %add_rsqrt_fusion.1) | copy-start | bytes 12292
  82.8 46.3 %copy-start.38 = (f32[768]{0:T(1024)}, f32[768]{0:T(1024)S(1)}, u32[]{:S(2)}) copy-start(f32[768]{0:T(1024)S(1)} %convert_element_type.200) | copy-start | bytes 9220
  85.4 2.6 collective-permute-start.12
  85.4 7.2 collective-permute-start.6
  88.0 6.6 collective-permute-start.13
  92.6 7.0 collective-permute-start.7
  94.5 15.5 %collective-permute-start.14 = (bf16[48,768]{1,0:T(8,128)(2,1)S(1)}, bf16[48,768]{1,0:T(8,128)(2,1)S(1)}, u32[]{:S(2)}, u32[]{:S(2)}) collective-permute-start(bf16[48,768]{1,0:T(8,128)(2,1)S(1)} %collective-permute-done.13), channel_id=1, source_target_pairs={{1,0},{2,1},{3,2},{4,3},{5,4},{6,5},{7,6},{8,7},{9,8},{10,9},{11,1... | collective-permute-start | bytes 221192 | tf_op jit(solution)/shard_map/ppermute | solution.py:29
  132.1 35.9 %copy-start.2 = (bf16[1,1024,12,32]{1,3,2,0:T(8,128)(2,1)}, bf16[1,1024,12,32]{1,3,2,0:T(8,128)(2,1)S(1)}, u32[]{:S(2)}) copy-start(bf16[1,1024,12,32]{1,3,2,0:T(8,128)(2,1)S(1)} %get-tuple-element.63) | copy-start | bytes 2359300
  132.1 35.9 %copy-start.4 = (bf16[1,1024,12,32]{1,3,2,0:T(8,128)(2,1)}, bf16[1,1024,12,32]{1,3,2,0:T(8,128)(2,1)S(1)}, u32[]{:S(2)}) copy-start(bf16[1,1024,12,32]{1,3,2,0:T(8,128)(2,1)S(1)} %get-tuple-element.64) | copy-start | bytes 2359300
  132.2 35.9 %copy-start.9 = (bf16[1024,12,32]{0,2,1:T(8,128)(2,1)}, bf16[1024,12,32]{0,2,1:T(8,128)(2,1)S(1)}, u32[]{:S(2)}) copy-start(bf16[1024,12,32]{0,2,1:T(8,128)(2,1)S(1)} %get-tuple-element.57) | copy-start | bytes 2359300
  142.9 15.5 %copy-start = (f32[12,512,1024]{2,1,0:T(8,128)S(1)}, f32[12,512,1024]{2,1,0:T(8,128)}, u32[]{:S(2)}) copy-start(f32[12,512,1024]{2,1,0:T(8,128)} %get-tuple-element.74) | copy-start | bytes 75497472
  180.2 15.6 %copy-start.1 = (f32[12,512,1024]{2,1,0:T(8,128)S(1)}, f32[12,512,1024]{2,1,0:T(8,128)}, u32[]{:S(2)}) copy-start(f32[12,512,1024]{2,1,0:T(8,128)} %get-tuple-element.76) | copy-start | bytes 75497472
  272.3 14.4 %copy-start.43 = (bf16[768,2048]{1,0:T(8,128)(2,1)S(1)}, bf16[768,2048]{1,0:T(8,128)(2,1)}, u32[]{:S(2)}) copy-start(bf16[768,2048]{1,0:T(8,128)(2,1)} %all-gather.14.cloned.1.call-done) | copy-start | bytes 9437188
  301.7 12.0 %copy-start.27 = (bf16[1024,768]{0,1:T(8,128)(2,1)}, bf16[1024,768]{0,1:T(8,128)(2,1)S(1)}, u32[]{:S(2)}) copy-start(bf16[1024,768]{0,1:T(8,128)(2,1)S(1)} %convolution_convert_fusion.1) | copy-start | bytes 4718596
  313.6 13.1 %copy-start.37 = (f32[1024]{0:T(1024)S(1)}, f32[1024]{0:T(1024)}, u32[]{:S(2)}) copy-start(f32[1024]{0:T(1024)} %copy-done.36) | copy-start | bytes 12292
  313.7 13.1 %copy-start.39 = (f32[768]{0:T(1024)S(1)}, f32[768]{0:T(1024)}, u32[]{:S(2)}) copy-start(f32[768]{0:T(1024)} %copy-done.38) | copy-start | bytes 9220
  334.9 206.0 %reduce-scatter.12.cloned.1.call-start = ((), (), s32[]{:S(2)}) async-start(), calls=%async_computation.16 | async-start | bytes 2506752 | tf_op jit(solution)/shard_map/reduce_scatter | solution.py:267
  371.5 171.0 %reduce-scatter.8.cloned.1.call-start = ((), (), s32[]{:S(2)}) async-start(), calls=%async_computation.14 | async-start | bytes 2506752 | tf_op jit(solution)/shard_map/reduce_scatter | solution.py:265
  371.5 42.8 %copy-start.3 = (bf16[1,1024,12,32]{1,3,2,0:T(8,128)(2,1)S(1)}, bf16[1,1024,12,32]{1,3,2,0:T(8,128)(2,1)}, u32[]{:S(2)}) copy-start(bf16[1,1024,12,32]{1,3,2,0:T(8,128)(2,1)} %copy-done.2) | copy-start | bytes 2359300
  371.5 42.8 %copy-start.5 = (bf16[1,1024,12,32]{1,3,2,0:T(8,128)(2,1)S(1)}, bf16[1,1024,12,32]{1,3,2,0:T(8,128)(2,1)}, u32[]{:S(2)}) copy-start(bf16[1,1024,12,32]{1,3,2,0:T(8,128)(2,1)} %copy-done.4) | copy-start | bytes 2359300
  453.8 141.4 %reduce-scatter.10.cloned.1.call-start = ((), (), s32[]{:S(2)}) async-start(), calls=%async_computation.15 | async-start | bytes 2506752 | tf_op jit(solution)/shard_map/reduce_scatter | solution.py:266
  458.0 225.2 %reduce-scatter.18.cloned.1.call-start = ((), (), s32[]{:S(2)}) async-start(), calls=%async_computation.19 | async-start | bytes 6684672 | tf_op jit(solution)/shard_map/reduce_scatter | solution.py:271
  465.6 306.8 %reduce-scatter.16.cloned.1.call-start = ((), (), s32[]{:S(2)}) async-start(), calls=%async_computation.18 | async-start | bytes 6684672 | tf_op jit(solution)/shard_map/reduce_scatter | solution.py:270
  473.2 387.3 %reduce-scatter.20.cloned.1.call-start = ((), (), s32[]{:S(2)}) async-start(), calls=%async_computation.20 | async-start | bytes 6684672 | tf_op jit(solution)/shard_map/reduce_scatter | solution.py:272
  483.1 418.2 %all-reduce.10.cloned.1.call-start = ((), (), s32[]{:S(2)}) async-start(), calls=%async_computation.21 | async-start | bytes 1769472 | tf_op jit(solution)/shard_map/psum | solution.py:276
  (30 other events, 136.7 us)
Sparse Core Ops, SparseCore 0:
  10.3 42.7 all-gather.7
  55.3 38.4 all-gather.9
  96.1 37.4 all-gather.11
  135.8 44.1 all-gather.15
  182.1 43.9 all-gather.13
  228.3 43.9 all-gather.17
  274.6 37.1 all-gather.19
  335.0 61.8 reduce-scatter.13
  401.1 61.9 reduce-scatter.11
  466.7 62.0 reduce-scatter.7
  533.0 62.1 reduce-scatter.9
  599.0 84.2 reduce-scatter.17
  687.7 84.6 reduce-scatter.15
  776.2 84.3 reduce-scatter.19
  864.5 36.7 all-reduce.9
